TPU v7x, 32 devices: a whole 2x2x4 slice. The times are simulated.
32 devices in a mesh: rot: 8 (over y, x, core), az: 4 (over z).
Axes of the slice: x: 2, y: 2, z: 4, core: 2. Of those that a mesh axis runs over, the one named last changes fastest.
Arguments:
- inputs: bfloat16 [16, 4, 128, 128], P('rot', None, 'az'), may hold values from -6 to 6
- pre_one: bfloat16 [16, 4, 128, 128], P('rot', None, 'az'), may hold values from -8 to 8
- pre_two: bfloat16 [16, 4, 128, 128], P('rot', None, 'az'), may hold values from -8 to 8
- cotangent: bfloat16 [16, 4, 128, 128], P('rot', None, 'az'), may hold values from -6 to 6
- filt_one: bfloat16 [16, 3, 3, 128, 128], P('rot'), may hold values from -0.046875 to 0.046875
- filt_two: bfloat16 [16, 3, 3, 128, 128], P('rot'), may hold values from -0.046875 to 0.046875
Outputs:
- input_grad: bfloat16 [16, 4, 128, 128], P('rot', None, 'az')
- filt_grad_one: float32 [16, 3, 3, 128, 128], P('rot')
- filt_grad_two: float32 [16, 3, 3, 128, 128], P('rot')
All inputs are finite; a program needn't handle non-finite values.
Results may differ from a plain program's by a relative error of at most 0.018.
Values may be sent and summed in bfloat16 or wider, within the bound.
A program may use at most 64 MiB of HBM per device.

v0:
```python
import jax
import jax.numpy as jnp
from jax import lax
from jax.sharding import PartitionSpec as P


def with_halo(block, sides, width):
    for axis, dim in sides:
        count = lax.axis_size(axis)
        forward = [(i, i + 1) for i in range(count - 1)]
        forward.append((count - 1, 0))
        backward = [(target, source) for source, target in forward]
        low = lax.ppermute(
            lax.slice_in_dim(block, block.shape[dim] - width, None, axis=dim), axis, forward
        )
        high = lax.ppermute(lax.slice_in_dim(block, 0, width, axis=dim), axis, backward)
        block = jnp.concatenate([low, block, high], axis=dim)
    return block


def slope(pre):
    widened = pre.astype(jnp.float32)
    logistic = jax.nn.sigmoid(widened)
    return logistic * (1.0 + widened * (1.0 - logistic))


def pad_rows(field):
    return jnp.pad(field, ((0, 0), (1, 1), (0, 0), (0, 0)))


def doubled_rows(field):
    padded = pad_rows(field)
    return jnp.concatenate([padded, padded], axis=0)


def filter_terms(features, gradient, my_rank, per_dev):
    doubled = doubled_rows(features)
    orient_count = gradient.shape[0]
    row_count = gradient.shape[1]
    col_count = gradient.shape[2]
    channels = gradient.shape[3]
    results = []
    for slot_index in range(per_dev):
        shifted = lax.dynamic_slice_in_dim(doubled, my_rank * per_dev + slot_index, orient_count, 0)
        pieces = []
        for row_tap in range(3):
            for col_tap in range(3):
                window = shifted[:, row_tap : row_tap + row_count, col_tap : col_tap + col_count, :]
                pieces.append(
                    lax.dot_general(
                        window,
                        gradient,
                        (((0, 1, 2), (0, 1, 2)), ((), ())),
                        preferred_element_type=jnp.float32,
                    )
                )
        results.append(jnp.stack(pieces).reshape(3, 3, channels, channels))
    return jnp.stack(results)


def make_terms(doubled, my_rank, filt_local, row_count, col_count, first_row, row_span):
    orient_count = doubled.shape[0] // 2
    channels = doubled.shape[3]
    per_dev = filt_local.shape[0]
    summed = jnp.zeros((row_span, row_count, col_count, channels), jnp.float32)
    for slot_index in range(per_dev):
        relative = my_rank * per_dev + slot_index
        offset = (first_row - relative) % orient_count
        chosen = lax.dynamic_slice_in_dim(doubled, offset, row_span, 0)
        for row_tap in range(3):
            for col_tap in range(3):
                window = chosen[
                    :,
                    2 - row_tap : 2 - row_tap + row_count,
                    2 - col_tap : 2 - col_tap + col_count,
                    :,
                ]
                summed = summed + lax.dot_general(
                    window,
                    filt_local[slot_index, row_tap, col_tap],
                    (((3,), (1,)), ((), ())),
                    preferred_element_type=jnp.float32,
                )
    return summed


def shards(inputs, pre_one, pre_two, cotangent, filt_one, filt_two):
    per_dev = inputs.shape[0]
    row_count = inputs.shape[1]
    col_count = inputs.shape[2]
    my_rank = lax.axis_index("rot")
    cell_count = per_dev * lax.axis_size("rot") * row_count * col_count * lax.axis_size("az")
    norm_scale = cell_count ** (-0.5)
    act_one = jax.nn.silu(pre_one.astype(jnp.float32)).astype(jnp.bfloat16)
    grad_two = (cotangent.astype(jnp.float32) * slope(pre_two)).astype(jnp.bfloat16)
    stacked = jnp.concatenate([inputs, act_one, grad_two], axis=0)
    widened = with_halo(stacked, (("az", 2),), 1)
    inputs_rim = widened[0:per_dev]
    act_rim = widened[per_dev : 2 * per_dev]
    grad_rim = widened[2 * per_dev : 3 * per_dev]
    all_inputs, all_act, all_grad = (
        lax.all_gather(inputs_rim, "rot", axis=0, tiled=True),
        lax.all_gather(act_rim, "rot", axis=0, tiled=True),
        lax.all_gather(grad_rim, "rot", axis=0, tiled=True),
    )
    out_cols = all_grad.shape[2] - 2
    margin = (all_grad.shape[2] - col_count) // 2
    doubled_two = doubled_rows(all_grad)
    delta_one = lax.psum_scatter(
        make_terms(
            doubled_two,
            my_rank,
            filt_two,
            row_count,
            out_cols,
            jnp.int32(0),
            per_dev * lax.axis_size("rot"),
        ),
        "rot",
        scatter_dimension=0,
        tiled=True,
    )
    grad_inner = all_grad[:, :, margin : margin + col_count]
    filt_part_two = filter_terms(all_act, grad_inner, my_rank, per_dev)
    grad_one = (delta_one * slope(pre_one)).astype(jnp.bfloat16)
    grad_one_rim = with_halo(grad_one, (("az", 2),), 1)
    all_grad_one = lax.all_gather(grad_one_rim, "rot", axis=0, tiled=True)
    doubled_one = doubled_rows(all_grad_one)
    input_sum = lax.psum_scatter(
        make_terms(
            doubled_one,
            my_rank,
            filt_one,
            row_count,
            col_count,
            jnp.int32(0),
            lax.axis_size("rot") * per_dev,
        ).astype(jnp.bfloat16),
        "rot",
        scatter_dimension=0,
        tiled=True,
    )
    filt_part_one = filter_terms(all_inputs, all_grad_one[:, :, 1:-1], my_rank, per_dev)
    summed_one, summed_two = (
        lax.psum(filt_part_one.astype(jnp.bfloat16), "az").astype(jnp.float32),
        lax.psum(filt_part_two.astype(jnp.bfloat16), "az").astype(jnp.float32),
    )
    return (input_sum, summed_one * norm_scale, summed_two * norm_scale)


def solution(mesh):
    return jax.shard_map(
        shards,
        mesh=mesh,
        in_specs=(
            P("rot", None, "az", None),
            P("rot", None, "az", None),
            P("rot", None, "az", None),
            P("rot", None, "az", None),
            P("rot", None, None, None, None),
            P("rot", None, None, None, None),
        ),
        out_specs=(
            P("rot", None, "az", None),
            P("rot", None, None, None, None),
            P("rot", None, None, None, None),
        ),
        check_vma=False,
    )
```

profile of v0, /device:TPU:0, one launch (start us, length us, event | category | flops | bytes accessed | tf_op | source)
XLA Modules:
  0.0 203.7 jit_solution(10225011640854622660)
XLA Ops:
  7.2 1.0 fusion.197
  8.2 0.8 pad_maximum_fusion.6
  9.0 5.1 %collective-permute-start.1 = (bf16[6,4,1,128]{3,2,1,0:T(2,128)(2,1)S(1)}, bf16[6,4,1,128]{3,2,1,0:T(2,128)(2,1)S(1)}, u32[]{:S(2)}, u32[]{:S(2)}) collective-permute-start(bf16[6,4,1,128]{3,2,1,0:T(2,128)(2,1)S(1)} %get-tuple-element.17), channel_id=1, source_target_pairs={{1,0},{2,1},{3,2},{0,3},{5,4},{6,5},{7,6},{4,7},{9,8},{10,9},{11,1... | collective-permute-start | bytes 18440 | tf_op jit(solution)/shard_map/ppermute | solution.py:16
  14.1 1.4 collective-permute-done.1
  15.5 4.1 %collective-permute-done = bf16[6,4,1,128]{3,2,1,0:T(2,128)(2,1)S(1)} collective-permute-done((bf16[6,4,1,128]{3,2,1,0:T(2,128)(2,1)S(1)}, bf16[6,4,1,128]{3,2,1,0:T(2,128)(2,1)S(1)}, u32[]{:S(2)}, u32[]{:S(2)}) %collective-permute-start) | collective-permute-done | bytes 6176 | tf_op jit(solution)/shard_map/ppermute | solution.py:13
  19.6 1.0 pad_maximum_fusion.2
  20.6 10.0 %all_gather.12 = bf16[16,4,34,128]{3,1,2,0:T(4,128)(2,1)S(1)} all-gather(bf16[2,4,34,128]{3,1,2,0:T(4,128)(2,1)S(1)} %copy.9), channel_id=1, replica_groups=mesh['rot'=8,'az'=4] {'rot'}, dimensions={0}, use_global_device_ids=true | all-gather | bytes 626688 | tf_op jit(solution)/shard_map/all_gather | solution.py:104
  30.8 0.8 fusion.115
  37.3 1.3 convolution_add_fusion.17
  38.7 10.0 %all_gather.14 = bf16[16,4,34,128]{3,1,2,0:T(4,128)(2,1)S(1)} all-gather(bf16[2,4,34,128]{3,1,2,0:T(4,128)(2,1)S(1)} %copy.13), channel_id=1, replica_groups=mesh['rot'=8,'az'=4] {'rot'}, dimensions={0}, use_global_device_ids=true | all-gather | bytes 626688 | tf_op jit(solution)/shard_map/all_gather | solution.py:102
  48.9 9.2 %all_gather.15 = bf16[16,4,34,128]{3,1,2,0:T(4,128)(2,1)S(1)} all-gather(bf16[2,4,34,128]{3,1,2,0:T(4,128)(2,1)S(1)} %copy.16), channel_id=1, replica_groups=mesh['rot'=8,'az'=4] {'rot'}, dimensions={0}, use_global_device_ids=true | all-gather | bytes 626688 | tf_op jit(solution)/shard_map/all_gather | solution.py:103
  58.3 0.8 fusion.110
  59.4 0.4 fusion.52
  59.8 0.4 fusion.50
  60.3 0.4 fusion.48
  60.6 0.4 fusion.46
  61.1 0.4 fusion.44
  61.5 0.4 fusion.42
  61.9 0.4 fusion.40
  62.3 0.4 fusion.38
  63.1 0.4 fusion.70
  63.5 0.4 fusion.68
  64.0 1.7 fusion.112
  65.7 0.4 fusion.66
  66.0 0.4 fusion.64
  66.5 0.4 fusion.62
  66.9 0.4 fusion.60
  67.3 0.4 fusion.58
  67.7 0.4 fusion.56
  68.1 3.8 %reduce-scatter.3.cloned.1.call-done = f32[2,4,32,128]{3,2,1,0:T(8,128)} async-done(((f32[16,4,32,128]{3,2,1,0:T(8,128)}), f32[2,4,32,128]{3,2,1,0:T(8,128)}) %reduce-scatter.3.cloned.1.call-update) | async-done | bytes 131088 | tf_op jit(solution)/shard_map/reduce_scatter | solution.py:109
  72.0 1.0 fusion.205
  73.0 3.4 %collective-permute-start.3 = (bf16[2,4,1,128]{3,2,1,0:T(2,128)(2,1)S(1)}, bf16[2,4,1,128]{3,2,1,0:T(2,128)(2,1)S(1)}, u32[]{:S(2)}, u32[]{:S(2)}) collective-permute-start(bf16[2,4,1,128]{3,2,1,0:T(2,128)(2,1)S(1)} %get-tuple-element.19), channel_id=1, source_target_pairs={{1,0},{2,1},{3,2},{0,3},{5,4},{6,5},{7,6},{4,7},{9,8},{10,9},{11,1... | collective-permute-start | bytes 6152 | tf_op jit(solution)/shard_map/ppermute | solution.py:16
  76.3 0.9 pad_maximum_fusion.1
  77.2 0.4 collective-permute-done.3
  77.7 4.1 %collective-permute-done.2 = bf16[2,4,1,128]{3,2,1,0:T(2,128)(2,1)S(1)} collective-permute-done((bf16[2,4,1,128]{3,2,1,0:T(2,128)(2,1)S(1)}, bf16[2,4,1,128]{3,2,1,0:T(2,128)(2,1)S(1)}, u32[]{:S(2)}, u32[]{:S(2)}) %collective-permute-start.2) | collective-permute-done | bytes 2080 | tf_op jit(solution)/shard_map/ppermute | solution.py:13
  81.8 10.2 %all_gather.13 = bf16[16,4,34,128]{3,1,2,0:T(4,128)(2,1)S(1)} all-gather(bf16[2,4,34,128]{3,1,2,0:T(4,128)(2,1)S(1)} %copy.11), channel_id=1, replica_groups=mesh['rot'=8,'az'=4] {'rot'}, dimensions={0}, use_global_device_ids=true | all-gather | bytes 626688 | tf_op jit(solution)/shard_map/all_gather | solution.py:127
  92.2 0.8 fusion.113
  97.4 0.9 copy-done
  98.6 0.4 fusion.88
  99.0 0.4 fusion.86
  99.5 0.4 fusion.84
  99.8 0.4 fusion.82
  100.3 0.4 fusion.80
  100.7 0.4 fusion.78
  101.1 0.4 fusion.76
  101.5 0.4 fusion.74
  102.3 0.4 fusion.106
  102.7 0.4 fusion.104
  103.2 0.4 fusion.102
  103.5 0.4 fusion.100
  103.9 0.4 fusion.98
  104.4 0.4 fusion.96
  104.7 0.4 fusion.94
  105.2 0.4 fusion.92
  105.6 0.9 pad_maximum_fusion
  106.6 1.1 convolution_add_fusion.4
  107.7 1.1 convolution_add_fusion.3
  108.7 1.1 convolution_add_fusion.2
  109.8 1.1 convolution_add_fusion.1
  110.9 1.9 fusion
  112.8 47.2 %all-reduce.7.cloned.1.call-done = (bf16[2,3,3,128,128]{4,3,2,1,0:T(8,128)(2,1)}, bf16[2,3,3,128,128]{4,3,2,1,0:T(8,128)(2,1)}) async-done(((bf16[2,3,3,128,128]{4,3,2,1,0:T(8,128)(2,1)}, bf16[2,3,3,128,128]{4,3,2,1,0:T(8,128)(2,1)}), (bf16[2,3,3,128,128]{4,3,2,1,0:T(8,128)(2,1)}, bf16[2,3,3,128,128]{4,3,2,1,0:T(8,128)(2,1)})) %all-reduce.7.cloned.1.call-update) | async-done | bytes 1179664 | tf_op jit(solution)/shard_map/psum | solution.py:145
  159.9 2.3 %convert_multiply_fusion.1 = f32[2,3,3,128,128]{4,3,2,1,0:T(8,128)} fusion(bf16[2,3,3,128,128]{4,3,2,1,0:T(8,128)(2,1)} %get-tuple-element.3), kind=kLoop, calls=%fused_computation.52 | loop fusion | flops 589824 | bytes 1769472 | tf_op jit(solution)/shard_map/mul | solution.py:148
  162.2 1.2 convert_multiply_fusion
  163.4 33.8 %reduce-scatter.5.cloned.1.call-done = bf16[2,4,32,128]{3,2,1,0:T(8,128)(2,1)} async-done(((bf16[16,4,32,128]{3,2,1,0:T(8,128)(2,1)}), bf16[2,4,32,128]{3,2,1,0:T(8,128)(2,1)}) %reduce-scatter.5.cloned.1.call-update) | async-done | bytes 65552 | tf_op jit(solution)/shard_map/reduce_scatter | solution.py:129
  (66 shorter events, 12.4 us)
Async XLA Ops:
  7.2 64.8 %reduce-scatter.3.cloned.1.call-start = ((), (), s32[]{:S(2)}) async-start(), calls=%async_computation.2 | async-start | bytes 1179648 | tf_op jit(solution)/shard_map/reduce_scatter | solution.py:109
  9.0 6.5 %collective-permute-start.1 = (bf16[6,4,1,128]{3,2,1,0:T(2,128)(2,1)S(1)}, bf16[6,4,1,128]{3,2,1,0:T(2,128)(2,1)S(1)}, u32[]{:S(2)}, u32[]{:S(2)}) collective-permute-start(bf16[6,4,1,128]{3,2,1,0:T(2,128)(2,1)S(1)} %get-tuple-element.17), channel_id=1, source_target_pairs={{1,0},{2,1},{3,2},{0,3},{5,4},{6,5},{7,6},{4,7},{9,8},{10,9},{11,1... | collective-permute-start | bytes 18440 | tf_op jit(solution)/shard_map/ppermute | solution.py:16
  14.1 5.5 %collective-permute-start = (bf16[6,4,1,128]{3,2,1,0:T(2,128)(2,1)S(1)}, bf16[6,4,1,128]{3,2,1,0:T(2,128)(2,1)S(1)}, u32[]{:S(2)}, u32[]{:S(2)}) collective-permute-start(bf16[6,4,1,128]{3,2,1,0:T(2,128)(2,1)S(1)} %get-tuple-element.16), channel_id=1, source_target_pairs={{0,1},{1,2},{2,3},{3,0},{4,5},{5,6},{6,7},{7,4},{8,9},{9,10},{10,1... | collective-permute-start | bytes 18440 | tf_op jit(solution)/shard_map/ppermute | solution.py:13
  30.8 1.1 copy-start.3
  38.6 121.4 %all-reduce.7.cloned.1.call-start = ((), (), s32[]{:S(2)}) async-start(), calls=%async_computation.4 | async-start | bytes 2359296 | tf_op jit(solution)/shard_map/psum | solution.py:145
  67.7 4.3 %copy-start.4 = (bf16[2,4,32,128]{3,2,1,0:T(8,128)(2,1)S(1)}, bf16[2,4,32,128]{3,2,1,0:T(8,128)(2,1)}, u32[]{:S(2)}) copy-start(bf16[2,4,32,128]{3,2,1,0:T(8,128)(2,1)} %param.7) | copy-start | bytes 196612
  73.0 4.7 %collective-permute-start.3 = (bf16[2,4,1,128]{3,2,1,0:T(2,128)(2,1)S(1)}, bf16[2,4,1,128]{3,2,1,0:T(2,128)(2,1)S(1)}, u32[]{:S(2)}, u32[]{:S(2)}) collective-permute-start(bf16[2,4,1,128]{3,2,1,0:T(2,128)(2,1)S(1)} %get-tuple-element.19), channel_id=1, source_target_pairs={{1,0},{2,1},{3,2},{0,3},{5,4},{6,5},{7,6},{4,7},{9,8},{10,9},{11,1... | collective-permute-start | bytes 6152 | tf_op jit(solution)/shard_map/ppermute | solution.py:16
  76.3 5.4 %collective-permute-start.2 = (bf16[2,4,1,128]{3,2,1,0:T(2,128)(2,1)S(1)}, bf16[2,4,1,128]{3,2,1,0:T(2,128)(2,1)S(1)}, u32[]{:S(2)}, u32[]{:S(2)}) collective-permute-start(bf16[2,4,1,128]{3,2,1,0:T(2,128)(2,1)S(1)} %get-tuple-element.18), channel_id=1, source_target_pairs={{0,1},{1,2},{2,3},{3,0},{4,5},{5,6},{6,7},{7,4},{8,9},{9,10},{10,1... | collective-permute-start | bytes 6152 | tf_op jit(solution)/shard_map/ppermute | solution.py:13
  92.2 1.1 copy-start.2
  97.0 1.2 copy-start
  106.5 90.6 %reduce-scatter.5.cloned.1.call-start = ((), (), s32[]{:S(2)}) async-start(), calls=%async_computation.3 | async-start | bytes 589824 | tf_op jit(solution)/shard_map/reduce_scatter | solution.py:129
  159.9 2.3 %copy-start.1 = (bf16[2,3,3,128,128]{4,3,2,1,0:T(8,128)(2,1)S(1)}, bf16[2,3,3,128,128]{4,3,2,1,0:T(8,128)(2,1)}, u32[]{:S(2)}) copy-start(bf16[2,3,3,128,128]{4,3,2,1,0:T(8,128)(2,1)} %get-tuple-element.4) | copy-start | bytes 1769476
Sparse Core Ops, SparseCore 0:
  38.7 33.2 reduce-scatter.2
  106.6 53.2 all-reduce.6
  163.6 33.5 reduce-scatter.4
where the time goes:
time: 205 us; the launch traced here: 204 us
  waiting for transfers between devices  94.8 us (46%)
  blocking collectives  39.3 us (19%)
  matrix products  31.5 us (15%)
  between operations  14.1 us (7%)
  other arithmetic  13 us (6%)
  starting transfers between devices  8.63 us (4%)
  local copies, waits for them, and re-layouts  2.34 us (1%)
    psum x1, waiting for transfers between devices, shards(): lax.psum(filt_part_one.astype(jnp.bfloat16), 'az').astype(jnp.float32)  47.2 us
    reduce_scatter x1, waiting for transfers between devices, shards(): lax.psum_scatter(make_terms(doubled_one, my_rank, filt_one, row_count, co...  33.8 us
    dot_general x36, matrix products, make_terms(): lax.dot_general(window, filt_local[slot_index, row_tap, col_tap], (((3,),...  16.8 us
    dot_general x36, matrix products, filter_terms(): lax.dot_general(window, gradient, (((0, 1, 2), (0, 1, 2)), ((), ())), pre...  14.7 us
    all_gather x1, blocking collectives, shards(): all_grad_one = lax.all_gather(grad_one_rim, 'rot', axis=0, tiled=True)  10.2 us
    all_gather x1, blocking collectives, shards(): lax.all_gather(grad_rim, 'rot', axis=0, tiled=True)  9.99 us
    all_gather x1, blocking collectives, shards(): lax.all_gather(inputs_rim, 'rot', axis=0, tiled=True)  9.96 us
    all_gather x1, blocking collectives, shards(): lax.all_gather(act_rim, 'rot', axis=0, tiled=True)  9.19 us
  transfers between devices with their start and end apart: 7, of which 7 were waited for; matrix products, arithmetic and copies ran while one was open for 10% of the time, Pallas kernels for 0%

commit v1 on v0

--- a/solution.py
+++ b/solution.py
@@ -142,7 +142,9 @@
     )
     filt_part_one = filter_terms(all_inputs, all_grad_one[:, :, 1:-1], my_rank, per_dev)
     summed_one, summed_two = (
-        lax.psum(filt_part_one.astype(jnp.bfloat16), "az").astype(jnp.float32),
+        jnp.sum(lax.all_gather(filt_part_one.astype(jnp.bfloat16), "az"), axis=0).astype(
+            jnp.float32
+        ),
         lax.psum(filt_part_two.astype(jnp.bfloat16), "az").astype(jnp.float32),
     )
     return (input_sum, summed_one * norm_scale, summed_two * norm_scale)

time: 205 us -> 181 us (0.88)
  waiting for transfers between devices: 94.8 us -> 66.2 us
  other arithmetic: 13 us -> 15.4 us
    all_gather x0 -> x1, waiting for transfers between devices: none -> 49.1 us  [shards(): lax.all_gather(filt_part_one.astype(jnp.bfloat16), 'az')]
    psum x1, waiting for transfers between devices: 47.2 us -> 3.56 us  [shards(): lax.psum(filt_part_two.astype(jnp.bfloat16), 'az').astype(jnp.float32)]
    reduce_scatter x1, waiting for transfers between devices: 33.8 us -> 0.01 us  [shards(): lax.psum_scatter(make_terms(doubled_one, my_rank, filt_one, row_count, co...]
    reduce_sum x0 -> x1, other arithmetic: none -> 2.15 us  [shards(): jnp.sum(lax.all_gather(filt_part_one.astype(jnp.bfloat16), 'az'), axis=0)]
  transfers between devices with their start and end apart: 7 -> 8, of which waited for: 7 -> 7; matrix products, arithmetic and copies ran while one was open for 10% -> 21% of each run, Pallas kernels for 0% -> 0%
where the time goes in v1:
time: 181 us; the launch traced here: 180 us
  waiting for transfers between devices  66.2 us (37%)
  blocking collectives  39.3 us (22%)
  matrix products  32.3 us (18%)
  between operations  15.9 us (9%)
  other arithmetic  15.4 us (9%)
  starting transfers between devices  8.95 us (5%)
  local copies, waits for them, and re-layouts  1.93 us (1%)
    all_gather x1, waiting for transfers between devices, shards(): lax.all_gather(filt_part_one.astype(jnp.bfloat16), 'az')  49.1 us
    dot_general x36, matrix products, make_terms(): lax.dot_general(window, filt_local[slot_index, row_tap, col_tap], (((3,),...  17.7 us
    dot_general x36, matrix products, filter_terms(): lax.dot_general(window, gradient, (((0, 1, 2), (0, 1, 2)), ((), ())), pre...  14.7 us
    all_gather x1, blocking collectives, shards(): all_grad_one = lax.all_gather(grad_one_rim, 'rot', axis=0, tiled=True)  10.2 us
    all_gather x1, blocking collectives, shards(): lax.all_gather(grad_rim, 'rot', axis=0, tiled=True)  9.99 us
    all_gather x1, blocking collectives, shards(): lax.all_gather(inputs_rim, 'rot', axis=0, tiled=True)  9.96 us
    all_gather x1, blocking collectives, shards(): lax.all_gather(act_rim, 'rot', axis=0, tiled=True)  9.18 us
    ppermute x2, starting transfers between devices, with_halo(): lax.ppermute(lax.slice_in_dim(block, 0, width, axis=dim), axis, backward)  8.51 us
  transfers between devices with their start and end apart: 8, of which 7 were waited for; matrix products, arithmetic and copies ran while one was open for 21% of the time, Pallas kernels for 0%

profile of v1, /device:TPU:0, one launch (start us, length us, event | category | flops | bytes accessed | tf_op | source)
XLA Modules:
  0.0 180.0 jit_solution(15355442952701883251)
XLA Ops:
  8.0 1.0 fusion.197
  9.0 0.8 pad_maximum_fusion.6
  9.8 5.1 %collective-permute-start.1 = (bf16[6,4,1,128]{3,2,1,0:T(2,128)(2,1)S(1)}, bf16[6,4,1,128]{3,2,1,0:T(2,128)(2,1)S(1)}, u32[]{:S(2)}, u32[]{:S(2)}) collective-permute-start(bf16[6,4,1,128]{3,2,1,0:T(2,128)(2,1)S(1)} %get-tuple-element.15), channel_id=1, source_target_pairs={{1,0},{2,1},{3,2},{0,3},{5,4},{6,5},{7,6},{4,7},{9,8},{10,9},{11,1... | collective-permute-start | bytes 18440 | tf_op jit(solution)/shard_map/ppermute | solution.py:16
  14.9 1.4 collective-permute-done.1
  16.3 4.1 %collective-permute-done = bf16[6,4,1,128]{3,2,1,0:T(2,128)(2,1)S(1)} collective-permute-done((bf16[6,4,1,128]{3,2,1,0:T(2,128)(2,1)S(1)}, bf16[6,4,1,128]{3,2,1,0:T(2,128)(2,1)S(1)}, u32[]{:S(2)}, u32[]{:S(2)}) %collective-permute-start) | collective-permute-done | bytes 6176 | tf_op jit(solution)/shard_map/ppermute | solution.py:13
  20.4 1.0 pad_maximum_fusion.2
  21.5 10.0 %all_gather.16 = bf16[16,4,34,128]{3,1,2,0:T(4,128)(2,1)S(1)} all-gather(bf16[2,4,34,128]{3,1,2,0:T(4,128)(2,1)S(1)} %copy.9), channel_id=1, replica_groups=mesh['rot'=8,'az'=4] {'rot'}, dimensions={0}, use_global_device_ids=true | all-gather | bytes 626688 | tf_op jit(solution)/shard_map/all_gather | solution.py:104
  31.7 0.8 fusion.115
  38.0 1.3 convolution_add_fusion.17
  39.4 10.0 %all_gather.18 = bf16[16,4,34,128]{3,1,2,0:T(4,128)(2,1)S(1)} all-gather(bf16[2,4,34,128]{3,1,2,0:T(4,128)(2,1)S(1)} %copy.13), channel_id=1, replica_groups=mesh['rot'=8,'az'=4] {'rot'}, dimensions={0}, use_global_device_ids=true | all-gather | bytes 626688 | tf_op jit(solution)/shard_map/all_gather | solution.py:102
  49.6 9.2 %all_gather.20 = bf16[16,4,34,128]{3,1,2,0:T(4,128)(2,1)S(1)} all-gather(bf16[2,4,34,128]{3,1,2,0:T(4,128)(2,1)S(1)} %copy.16), channel_id=1, replica_groups=mesh['rot'=8,'az'=4] {'rot'}, dimensions={0}, use_global_device_ids=true | all-gather | bytes 626688 | tf_op jit(solution)/shard_map/all_gather | solution.py:103
  59.0 0.8 fusion.110
  60.1 0.4 fusion.52
  60.6 0.4 fusion.50
  61.4 0.4 fusion.46
  61.8 0.4 fusion.44
  62.2 0.4 fusion.42
  62.6 0.4 fusion.40
  63.0 0.4 fusion.38
  63.8 0.4 fusion.70
  64.3 0.4 fusion.68
  64.7 2.1 %fusion.112 = (bf16[16,6,34,128]{3,2,1,0:T(8,128)(2,1)}, bf16[16,6,34,128]{3,2,1,0:T(8,128)(2,1)}) fusion(s32[]{:T(128)S(6)} %select_n.35, bf16[16,6,34,128]{3,2,1,0:T(8,128)(2,1)S(1)} %pad.15, s32[]{:T(128)S(6)} %select_n.36), kind=kLoop, calls=%fused_computation.200 | loop fusion | flops 835584 | bytes 2506760 | tf_op jit(solution)/shard_map/concatenate | solution.py:33
  67.1 0.4 fusion.64
  67.5 0.4 fusion.62
  68.0 0.4 fusion.60
  68.3 0.4 fusion.58
  68.8 0.4 fusion.56
  69.2 3.5 %reduce-scatter.3.cloned.1.call-done = f32[2,4,32,128]{3,2,1,0:T(8,128)} async-done(((f32[16,4,32,128]{3,2,1,0:T(8,128)}), f32[2,4,32,128]{3,2,1,0:T(8,128)}) %reduce-scatter.3.cloned.1.call-update) | async-done | bytes 131088 | tf_op jit(solution)/shard_map/reduce_scatter | solution.py:109
  72.7 1.0 fusion.205
  73.7 3.4 %collective-permute-start.3 = (bf16[2,4,1,128]{3,2,1,0:T(2,128)(2,1)S(1)}, bf16[2,4,1,128]{3,2,1,0:T(2,128)(2,1)S(1)}, u32[]{:S(2)}, u32[]{:S(2)}) collective-permute-start(bf16[2,4,1,128]{3,2,1,0:T(2,128)(2,1)S(1)} %get-tuple-element.17), channel_id=1, source_target_pairs={{1,0},{2,1},{3,2},{0,3},{5,4},{6,5},{7,6},{4,7},{9,8},{10,9},{11,1... | collective-permute-start | bytes 6152 | tf_op jit(solution)/shard_map/ppermute | solution.py:16
  77.1 0.9 pad_maximum_fusion.1
  78.0 0.4 collective-permute-done.3
  78.4 4.1 %collective-permute-done.2 = bf16[2,4,1,128]{3,2,1,0:T(2,128)(2,1)S(1)} collective-permute-done((bf16[2,4,1,128]{3,2,1,0:T(2,128)(2,1)S(1)}, bf16[2,4,1,128]{3,2,1,0:T(2,128)(2,1)S(1)}, u32[]{:S(2)}, u32[]{:S(2)}) %collective-permute-start.2) | collective-permute-done | bytes 2080 | tf_op jit(solution)/shard_map/ppermute | solution.py:13
  82.6 10.2 %all_gather.17 = bf16[16,4,34,128]{3,1,2,0:T(4,128)(2,1)S(1)} all-gather(bf16[2,4,34,128]{3,1,2,0:T(4,128)(2,1)S(1)} %copy.11), channel_id=1, replica_groups=mesh['rot'=8,'az'=4] {'rot'}, dimensions={0}, use_global_device_ids=true | all-gather | bytes 626688 | tf_op jit(solution)/shard_map/all_gather | solution.py:127
  92.9 0.8 fusion.113
  93.7 1.1 fusion.170
  94.8 1.1 convolution_add_fusion.16
  95.9 1.1 convolution_add_fusion.15
  97.5 0.4 fusion.88
  97.9 0.4 fusion.86
  98.3 0.4 fusion.84
  98.7 0.4 fusion.82
  99.1 0.4 fusion.80
  99.9 0.4 fusion.76
  100.4 0.4 fusion.74
  100.8 0.8 copy-done
  101.9 0.4 fusion.106
  102.3 0.4 fusion.104
  102.8 0.4 fusion.102
  103.1 0.4 fusion.100
  103.6 0.4 fusion.98
  104.0 0.4 fusion.96
  104.4 0.4 fusion.94
  104.8 0.4 fusion.92
  105.2 0.9 pad_maximum_fusion
  106.1 1.1 convolution_add_fusion.14
  107.2 1.1 convolution_add_fusion.13
  108.6 1.1 convolution_add_fusion.12
  113.2 1.1 fusion
  114.4 3.6 %all-reduce.6.cloned.1.call-done = bf16[2,3,3,128,128]{4,3,2,1,0:T(8,128)(2,1)} async-done(((bf16[2,3,3,128,128]{4,3,2,1,0:T(8,128)(2,1)}), bf16[2,3,3,128,128]{4,3,2,1,0:T(8,128)(2,1)}) %all-reduce.6.cloned.1.call-update) | async-done | bytes 589840 | tf_op jit(solution)/shard_map/psum | solution.py:148
  117.9 2.2 %convert_multiply_fusion = f32[2,3,3,128,128]{4,3,2,1,0:T(8,128)} fusion(bf16[2,3,3,128,128]{4,3,2,1,0:T(8,128)(2,1)} %all-reduce.6.cloned.1.call-done), kind=kLoop, calls=%fused_computation.51 | loop fusion | flops 589824 | bytes 1769472 | tf_op jit(solution)/shard_map/mul | solution.py:150
  120.1 49.1 %all-gather.2.cloned.1.call-done = bf16[4,2,3,3,128,128]{5,4,3,2,1,0:T(8,128)(2,1)} async-done(((bf16[1,2,3,3,128,128]{5,4,3,2,1,0:T(8,128)(2,1)}), bf16[4,2,3,3,128,128]{5,4,3,2,1,0:T(8,128)(2,1)}) %all-gather.2.cloned.1.call-update) | async-done | bytes 2359312 | tf_op jit(solution)/shard_map/all_gather | solution.py:145
  169.3 2.2 %reduce_sum.12 = bf16[2,3,3,128,128]{4,3,2,1,0:T(8,128)(2,1)S(1)} reduce(bf16[4,2,3,3,128,128]{5,4,3,2,1,0:T(8,128)(2,1)} %all-gather.2.cloned.1.call-done, bf16[]{:T(256)} %constant.35.clone.1), dimensions={0}, to_apply=%region_2.3 | reduce | flops 884736 | bytes 2949122 | tf_op jit(solution)/shard_map/reduce_sum | solution.py:145
  171.4 1.2 convert_multiply_fusion.1
  (70 shorter events, 12.9 us)
Async XLA Ops:
  8.0 64.7 %reduce-scatter.3.cloned.1.call-start = ((), (), s32[]{:S(2)}) async-start(), calls=%async_computation.2 | async-start | bytes 1179648 | tf_op jit(solution)/shard_map/reduce_scatter | solution.py:109
  9.8 6.5 %collective-permute-start.1 = (bf16[6,4,1,128]{3,2,1,0:T(2,128)(2,1)S(1)}, bf16[6,4,1,128]{3,2,1,0:T(2,128)(2,1)S(1)}, u32[]{:S(2)}, u32[]{:S(2)}) collective-permute-start(bf16[6,4,1,128]{3,2,1,0:T(2,128)(2,1)S(1)} %get-tuple-element.15), channel_id=1, source_target_pairs={{1,0},{2,1},{3,2},{0,3},{5,4},{6,5},{7,6},{4,7},{9,8},{10,9},{11,1... | collective-permute-start | bytes 18440 | tf_op jit(solution)/shard_map/ppermute | solution.py:16
  14.9 5.5 %collective-permute-start = (bf16[6,4,1,128]{3,2,1,0:T(2,128)(2,1)S(1)}, bf16[6,4,1,128]{3,2,1,0:T(2,128)(2,1)S(1)}, u32[]{:S(2)}, u32[]{:S(2)}) collective-permute-start(bf16[6,4,1,128]{3,2,1,0:T(2,128)(2,1)S(1)} %get-tuple-element.14), channel_id=1, source_target_pairs={{0,1},{1,2},{2,3},{3,0},{4,5},{5,6},{6,7},{7,4},{8,9},{9,10},{10,1... | collective-permute-start | bytes 18440 | tf_op jit(solution)/shard_map/ppermute | solution.py:13
  31.6 1.1 copy-start.3
  39.3 78.6 %all-reduce.6.cloned.1.call-start = ((), (), s32[]{:S(2)}) async-start(), calls=%async_computation.5 | async-start | bytes 1179648 | tf_op jit(solution)/shard_map/psum | solution.py:148
  68.8 3.9 %copy-start.4 = (bf16[2,4,32,128]{3,2,1,0:T(8,128)(2,1)S(1)}, bf16[2,4,32,128]{3,2,1,0:T(8,128)(2,1)}, u32[]{:S(2)}) copy-start(bf16[2,4,32,128]{3,2,1,0:T(8,128)(2,1)} %param.7) | copy-start | bytes 196612
  73.7 4.7 %collective-permute-start.3 = (bf16[2,4,1,128]{3,2,1,0:T(2,128)(2,1)S(1)}, bf16[2,4,1,128]{3,2,1,0:T(2,128)(2,1)S(1)}, u32[]{:S(2)}, u32[]{:S(2)}) collective-permute-start(bf16[2,4,1,128]{3,2,1,0:T(2,128)(2,1)S(1)} %get-tuple-element.17), channel_id=1, source_target_pairs={{1,0},{2,1},{3,2},{0,3},{5,4},{6,5},{7,6},{4,7},{9,8},{10,9},{11,1... | collective-permute-start | bytes 6152 | tf_op jit(solution)/shard_map/ppermute | solution.py:16
  77.1 5.4 %collective-permute-start.2 = (bf16[2,4,1,128]{3,2,1,0:T(2,128)(2,1)S(1)}, bf16[2,4,1,128]{3,2,1,0:T(2,128)(2,1)S(1)}, u32[]{:S(2)}, u32[]{:S(2)}) collective-permute-start(bf16[2,4,1,128]{3,2,1,0:T(2,128)(2,1)S(1)} %get-tuple-element.16), channel_id=1, source_target_pairs={{0,1},{1,2},{2,3},{3,0},{4,5},{5,6},{6,7},{7,4},{8,9},{9,10},{10,1... | collective-permute-start | bytes 6152 | tf_op jit(solution)/shard_map/ppermute | solution.py:13
  78.0 91.3 %all-gather.2.cloned.1.call-start = ((), (), s32[]{:S(2)}) async-start(), calls=%async_computation.4 | async-start | bytes 2949120 | tf_op jit(solution)/shard_map/all_gather | solution.py:145
  95.9 1.2 copy-start.1
  100.4 1.2 copy-start
  108.3 64.3 %reduce-scatter.5.cloned.1.call-start = ((), (), s32[]{:S(2)}) async-start(), calls=%async_computation.3 | async-start | bytes 589824 | tf_op jit(solution)/shard_map/reduce_scatter | solution.py:129
  108.6 1.1 copy-start.2
Sparse Core Ops, SparseCore 0:
  39.4 33.2 reduce-scatter.2
  114.5 31.3 reduce-scatter.4
Sparse Core Ops, SparseCore 1:
  78.1 39.8 all-reduce.5
  119.9 49.3 all-gather.1
